TPU v7x, 256 devices: a whole 4x4x8 slice. The times are simulated.
256 devices in a mesh: seq: 16 (over z, core), tensor: 16 (over x, y).
Axes of the slice: x: 4, y: 4, z: 8, core: 2. Of those that a mesh axis runs over, the one named last changes fastest.
Arguments:
- tokens: bfloat16 [4096, 7168], P('seq', 'tensor')
- positions: int32 [4096], P('seq'), may hold values from 0 to 4095, as said below
- w_down_q: bfloat16 [7168, 1536], P('tensor')
- w_down_kv: bfloat16 [7168, 512], P('tensor')
- w_rope_key: bfloat16 [7168, 64], P('tensor'), may hold values from -0.0625 to 0.0625
- gain_query: float32 [1536], replicated, may hold values from 0.25 to 1.75
- gain_kv: float32 [512], replicated, may hold values from 0.25 to 1.75
- w_up_q: bfloat16 [1536, 12288], P(None, 'tensor')
- w_up_kv: bfloat16 [512, 16384], P(None, 'tensor')
Outputs:
- attended: bfloat16 [4096, 8192], P('seq', 'tensor')
Inputs may be any that keep to these rules, and one draw needn't show every extreme that they name: The positions of the window's 4096 tokens are 0 to 4095, each once, in runs of 16 consecutive values that start at multiples of 16.
All inputs are finite; a program needn't handle non-finite values.
Results may differ from a plain program's by a relative error of at most 0.012.
The roundings to bfloat16 on the way count: a program that leaves them out, or rounds other values in their place, can miss the bound.
Values may be sent and summed in bfloat16 or wider, within the bound.
A program may use at most 128 MiB of HBM per device.

v0:
```python
import jax
import jax.numpy as jnp
from jax import lax
from jax.sharding import PartitionSpec as P

NOPE = 128
ROPE = 64
VDIM = 128
HEAD_DEV = 4


epsilon = 1e-06


def angles(where_at, width):
    half = width // 2
    freq = 10000.0 ** (-(jnp.arange(half, dtype=jnp.float32) * 2.0 / width))
    return where_at.astype(jnp.float32)[:, None] * freq[None, :]


def rotate(vector, angle):
    half = vector.shape[-1] // 2
    first = vector[..., :half]
    second = vector[..., half:]
    cosine = jnp.cos(angle)
    sine = jnp.sin(angle)
    return jnp.concatenate(
        [first * cosine - second * sine, second * cosine + first * sine], axis=-1
    )


def body(tokens, positions, w_down_q, w_down_kv, w_rope_key, gain_query, gain_kv, w_up_q, w_up_kv):
    softmax_scale = (1.0 + 0.1 * jnp.log(40.0)) ** 2 / jnp.sqrt(jnp.float32(NOPE + ROPE))
    tok_rows = tokens.shape[0]
    part_q = jnp.dot(tokens, w_down_q, preferred_element_type=jnp.float32)
    part_kv = jnp.dot(tokens, w_down_kv, preferred_element_type=jnp.float32)
    part_rope = jnp.dot(tokens, w_rope_key, preferred_element_type=jnp.float32)
    slice_q, slice_kv = (
        lax.psum_scatter(part_q, "tensor", scatter_dimension=1, tiled=True),
        lax.psum_scatter(part_kv, "tensor", scatter_dimension=1, tiled=True),
    )
    shard = lax.axis_index("tensor")
    width_q = slice_q.shape[1]
    width_kv = slice_kv.shape[1]
    gain_q_part = lax.dynamic_slice_in_dim(gain_query, shard * width_q, width_q)
    gain_kv_part = lax.dynamic_slice_in_dim(gain_kv, shard * width_kv, width_kv)
    total_q, total_kv, rope_raw = lax.psum(
        (jnp.sum(slice_q * slice_q, axis=1), jnp.sum(slice_kv * slice_kv, axis=1), part_rope),
        "tensor",
    )
    inv_q = lax.rsqrt(total_q / gain_query.shape[0] + epsilon)
    inv_kv = lax.rsqrt(total_kv / gain_kv.shape[0] + epsilon)
    piece_q = (slice_q * inv_q[:, None] * gain_q_part).astype(jnp.bfloat16)
    piece_kv = (slice_kv * inv_kv[:, None] * gain_kv_part).astype(jnp.bfloat16)
    latent_q, latent_kv = (
        lax.all_gather(piece_q, "tensor", axis=1, tiled=True),
        lax.all_gather(piece_kv, "tensor", axis=1, tiled=True),
    )
    turn = angles(positions, ROPE)
    rope_key = rotate(rope_raw, turn).astype(jnp.bfloat16)
    query = jnp.dot(latent_q, w_up_q, preferred_element_type=jnp.float32).reshape(
        tok_rows, HEAD_DEV, NOPE + ROPE
    )
    query_nope = query[..., :NOPE].astype(jnp.bfloat16)
    query_rope = rotate(query[..., NOPE:], turn[:, None, :]).astype(jnp.bfloat16)
    keyval_local = jnp.dot(latent_kv, w_up_kv, preferred_element_type=jnp.float32).astype(
        jnp.bfloat16
    )
    keyval = lax.all_gather(keyval_local, "seq", axis=0, tiled=True)
    running = jnp.full((tok_rows, HEAD_DEV), -1e30, jnp.float32)
    total = jnp.zeros((tok_rows, HEAD_DEV), jnp.float32)
    accum = jnp.zeros((tok_rows, HEAD_DEV, VDIM), jnp.float32)
    count = keyval.shape[0]
    keyval = keyval.reshape(count, HEAD_DEV, NOPE + VDIM)
    key_nope = keyval[..., :NOPE]
    values = keyval[..., NOPE:]
    scores = jnp.einsum("qhd,khd->qhk", query_nope, key_nope, preferred_element_type=jnp.float32)
    scores = scores + jnp.einsum(
        "qhd,kd->qhk",
        query_rope,
        lax.all_gather(rope_key, "seq", axis=0, tiled=True),
        preferred_element_type=jnp.float32,
    )
    visible = (lax.all_gather(positions, "seq", axis=0, tiled=True)[None, :] <= positions[:, None])[
        :, None, :
    ]
    scores = jnp.where(visible, scores * softmax_scale, jnp.float32(-1e30))
    fresh = jnp.maximum(running, jnp.max(scores, axis=-1))
    factor = jnp.exp(running - fresh)
    weights = jnp.where(visible, jnp.exp(scores - fresh[..., None]), jnp.float32(0.0))
    total = total * factor + jnp.sum(weights, axis=-1)
    accum = accum * factor[..., None] + jnp.einsum(
        "qhk,khd->qhd", weights.astype(jnp.bfloat16), values, preferred_element_type=jnp.float32
    )
    mixed = accum / total[..., None]
    return mixed.astype(jnp.bfloat16).reshape(tok_rows, HEAD_DEV * VDIM)


def solution(mesh):
    in_specs = (
        P("seq", "tensor"),
        P("seq"),
        P("tensor", None),
        P("tensor", None),
        P("tensor", None),
        P(),
        P(),
        P(None, "tensor"),
        P(None, "tensor"),
    )
    out_specs = P("seq", "tensor")
    return jax.shard_map(body, mesh=mesh, in_specs=in_specs, out_specs=out_specs, check_vma=False)
```

profile of v0, /device:TPU:1, one launch (start us, length us, event | category | flops | bytes accessed | tf_op | source)
XLA Modules:
  0.0 397.5 jit_solution(3694636255678999204)
XLA Ops:
  6.5 2.4 fusion.41
  9.0 0.0 reduce-scatter.5.cloned.1.call-start
  9.1 3.4 fusion.42
  12.5 0.0 all-reduce.3.cloned.1.call-start
  12.5 1.8 fusion.44
  14.4 0.8 dynamic_slice.6
  15.2 76.3 %reduce-scatter.3.cloned.1.call-done = f32[256,32]{0,1:T(8,128)} async-done(((f32[256,512]{0,1:T(8,128)}), f32[256,32]{0,1:T(8,128)}) %reduce-scatter.3.cloned.1.call-update) | async-done | bytes 32784 | tf_op jit(solution)/shard_map/reduce_scatter | solution.py:40
  91.4 0.8 multiply_reduce_fusion.1
  92.2 81.8 %reduce-scatter.5.cloned.1.call-done = f32[256,96]{0,1:T(8,128)} async-done(((f32[256,1536]{0,1:T(8,128)}), f32[256,96]{0,1:T(8,128)}) %reduce-scatter.5.cloned.1.call-update) | async-done | bytes 98320 | tf_op jit(solution)/shard_map/reduce_scatter | solution.py:39
  174.0 0.9 multiply_reduce_fusion
  174.9 30.9 %all-reduce = (f32[256]{0:T(256)S(1)}, f32[256]{0:T(256)S(1)}) all-reduce(f32[256]{0:T(256)S(1)} %multiply_reduce_fusion.1, f32[256]{0:T(256)S(1)} %multiply_reduce_fusion), channel_id=1, replica_groups=mesh['seq'=16,'tensor'=16] {'tensor'}, use_global_device_ids=true, to_apply=%region_2.0 | all-reduce | flops 512 | bytes 4096 | tf_op jit(solution)/shard_map/psum | solution.py:47
  205.8 0.8 multiply_convert_fusion.1
  206.7 15.6 %all_gather.16 = bf16[256,512]{0,1:T(8,128)(2,1)S(1)} all-gather(bf16[256,32]{0,1:T(8,128)(2,1)S(1)} %multiply_convert_fusion.1), channel_id=1, replica_groups=mesh['seq'=16,'tensor'=16] {'tensor'}, dimensions={1}, use_global_device_ids=true | all-gather | bytes 278528 | tf_op jit(solution)/shard_map/all_gather | solution.py:57
  222.3 2.5 convolution_convert_fusion
  224.8 0.8 dynamic_slice.7
  225.6 31.9 %all-gather = s32[16,1,256]{2,1,0:T(1,128)S(1)} all-gather(s32[1,1,256]{2,1,0:T(1,128)S(1)} %bitcast.37), channel_id=1, replica_groups=mesh['seq'=16,'tensor'=16] {'seq'}, dimensions={0}, use_global_device_ids=true | all-gather | bytes 17408 | tf_op jit(solution)/shard_map/all_gather | solution.py:84
  257.5 1.9 broadcast_compare_fusion
  259.4 9.3 %all-reduce.3.cloned.1.call-done = f32[256,64]{0,1:T(8,128)} async-done(((f32[256,64]{0,1:T(8,128)}), f32[256,64]{0,1:T(8,128)}) %all-reduce.3.cloned.1.call-update) | async-done | bytes 65552 | tf_op jit(solution)/shard_map/psum | solution.py:47
  268.7 1.0 multiply_cosine_fusion
  269.7 24.0 %all_gather.19 = bf16[4096,64]{0,1:T(8,128)(2,1)} all-gather(bf16[256,64]{0,1:T(8,128)(2,1)S(1)} %pad_maximum_fusion), channel_id=1, replica_groups=mesh['seq'=16,'tensor'=16] {'seq'}, dimensions={0}, use_global_device_ids=true | all-gather | bytes 557056 | tf_op jit(solution)/shard_map/all_gather | solution.py:81
  293.7 1.0 multiply_convert_fusion
  294.7 20.5 %all_gather.18 = bf16[256,1536]{0,1:T(8,128)(2,1)S(1)} all-gather(bf16[256,96]{0,1:T(8,128)(2,1)S(1)} %multiply_convert_fusion), channel_id=1, replica_groups=mesh['seq'=16,'tensor'=16] {'tensor'}, dimensions={1}, use_global_device_ids=true | all-gather | bytes 835584 | tf_op jit(solution)/shard_map/all_gather | solution.py:56
  315.2 1.1 fusion.43
  316.3 0.9 copy-done.3
  317.2 11.4 %all-gather.3.cloned.1.call-done = bf16[4096,1024]{1,0:T(8,128)(2,1)} async-done(((bf16[256,1024]{1,0:T(8,128)(2,1)}), bf16[4096,1024]{1,0:T(8,128)(2,1)}) %all-gather.3.cloned.1.call-update) | async-done | bytes 8388624 | tf_op jit(solution)/shard_map/all_gather | solution.py:69
  328.6 14.5 %reshape.102 = bf16[4096,4,256]{2,1,0:T(4,128)(2,1)} reshape(bf16[4096,1024]{1,0:T(8,128)(2,1)} %all-gather.3.cloned.1.call-done) | data formatting | bytes 16777216 | tf_op jit(solution)/shard_map/reshape | solution.py:74
  343.1 7.1 %fusion.39 = (bf16[4096,4,128]{2,1,0:T(4,128)(2,1)}, bf16[4096,4,128]{2,1,0:T(4,128)(2,1)S(1)}) fusion(bf16[4096,4,256]{2,1,0:T(4,128)(2,1)} %reshape.102), kind=kLoop, calls=%fused_computation.43 | loop fusion | bytes 16777216 | tf_op jit(solution)/shard_map/slice | solution.py:76
  350.2 8.1 %fusion.10 = f32[4,4096,256]{2,1,0:T(8,128)} fusion(bf16[4096,4,128]{2,1,0:T(4,128)(2,1)S(1)} %get-tuple-element.8, f32[256,4,192]{0,2,1:T(8,128)S(1)} %bitcast.34), kind=kOutput, calls=%fused_computation.11 | convolution fusion | flops 1073741824 | bytes 21233664 | tf_op jit(solution)/shard_map/qhd,khd->qhk/dot_general | solution.py:77
  358.3 10.9 %fusion.40 = (f32[256,4]{0,1:T(4,128)S(1)}, f32[256,4,4096]{0,2,1:T(8,128)}) fusion(bf16[4096,64]{0,1:T(8,128)(2,1)S(1)} %copy-done.2, bf16[256,4,32]{0,2,1:T(8,128)(2,1)S(1)} %get-tuple-element.10, bf16[256,4,32]{0,2,1:T(8,128)(2,1)S(1)} %get-tuple-element.9, f32[4,4096,256]{2,1,0:T(8,128)} %fusion.10, pred[256,4096]{0,1:T(8,128)(4,1)S(1)} %broadcast_compare_fusion), kind=kOutput, calls=%fused_computation.44 | convolution fusion | flops 553909248 | bytes 35262464 | tf_op jit(solution)/shard_map/qhd,kd->qhk/dot_general | solution.py:78
  369.2 8.8 %fusion.2 = f32[256,4]{0,1:T(4,128)S(1)} fusion(f32[256,4,4096]{0,2,1:T(8,128)} %get-tuple-element.20, f32[256,4]{0,1:T(4,128)S(1)} %broadcast_maximum_fusion, pred[256,4096]{0,1:T(8,128)(4,1)S(1)} %broadcast_compare_fusion), kind=kLoop, calls=%fused_computation.4 | loop fusion | flops 12581888 | bytes 17833984 | tf_op jit(solution)/shard_map/reduce_sum | solution.py:91
  378.0 11.2 %fusion.27 = bf16[256,4,128]{0,2,1:T(8,128)(2,1)} fusion(f32[256,4,4096]{0,2,1:T(8,128)} %get-tuple-element.20, f32[256,4]{0,1:T(4,128)S(1)} %broadcast_maximum_fusion, pred[256,4096]{0,1:T(8,128)(4,1)S(1)} %broadcast_compare_fusion, bf16[4096,4,128]{2,1,0:T(4,128)(2,1)} %get-tuple-element.7, f32[256,4]{0,1:T(4,128)S(1)} %get-tuple-element.14, ...), kind=kOutput, calls=%fused_computation.18 | convolution fusion | flops 1086717952 | bytes 22294528 | tf_op jit(solution)/shard_map/qhk,khd->qhd/dot_general | solution.py:92
  389.2 1.8 copy.38
  (25 shorter events, 0.2 us)
Async XLA Ops:
  6.5 308.7 %copy-start = (bf16[1536,768]{1,0:T(8,128)(2,1)S(1)}, bf16[1536,768]{1,0:T(8,128)(2,1)}, u32[]{:S(2)}) copy-start(bf16[1536,768]{1,0:T(8,128)(2,1)} %param.16) | copy-start | bytes 7077892
  6.5 218.3 %copy-start.5 = (s32[256]{0:T(256)S(1)}, s32[256]{0:T(256)}, u32[]{:S(2)}) copy-start(s32[256]{0:T(256)} %param.10) | copy-start | bytes 3076
  6.5 84.9 %reduce-scatter.3.cloned.1.call-start = ((), (), s32[]{:S(2)}) async-start(), calls=%async_computation.2 | async-start | bytes 557056 | tf_op jit(solution)/shard_map/reduce_scatter | solution.py:40
  9.0 165.0 %reduce-scatter.5.cloned.1.call-start = ((), (), s32[]{:S(2)}) async-start(), calls=%async_computation.4 | async-start | bytes 1671168 | tf_op jit(solution)/shard_map/reduce_scatter | solution.py:39
  12.5 256.2 %all-reduce.3.cloned.1.call-start = ((), (), s32[]{:S(2)}) async-start(), calls=%async_computation.5 | async-start | bytes 131072 | tf_op jit(solution)/shard_map/psum | solution.py:47
  14.3 314.2 %all-gather.3.cloned.1.call-start = ((), (), s32[]{:S(2)}) async-start(), calls=%async_computation.3 | async-start | bytes 8912896 | tf_op jit(solution)/shard_map/all_gather | solution.py:69
  316.3 0.9 copy-start.3
  343.1 7.1 %copy-start.4 = (f32[256,768]{0,1:T(8,128)S(1)}, f32[256,768]{0,1:T(8,128)}, u32[]{:S(2)}) copy-start(f32[256,768]{0,1:T(8,128)} %copy-done.3) | copy-start | bytes 2359300
  350.2 8.1 %copy-start.2 = (bf16[4096,64]{0,1:T(8,128)(2,1)S(1)}, bf16[4096,64]{0,1:T(8,128)(2,1)}, u32[]{:S(2)}) copy-start(bf16[4096,64]{0,1:T(8,128)(2,1)} %all_gather.19) | copy-start | bytes 1572868
  377.9 13.0 %copy-start.1 = (bf16[1536,768]{1,0:T(8,128)(2,1)S(1)}, bf16[1536,768]{1,0:T(8,128)(2,1)}, u32[]{:S(2)}) copy-start(bf16[1536,768]{1,0:T(8,128)(2,1)} %param.16) | copy-start | bytes 7077892
Sparse Core Ops, SparseCore 0:
  10.8 80.5 reduce-scatter.2
  94.9 79.0 reduce-scatter.4
  177.2 91.4 all-reduce.2
  270.4 58.1 all-gather.2
where the time goes:
time: 399 us; the launch traced here: 397 us
  waiting for transfers between devices  179 us (45%)
  blocking collectives  123 us (31%)
  matrix products  41.4 us (10%)
  local copies, waits for them, and re-layouts  25.9 us (6%)
  other arithmetic  15.2 us (4%)
  between operations  13.2 us (3%)
    reduce_scatter x1, waiting for transfers between devices, body(): lax.psum_scatter(part_q, 'tensor', scatter_dimension=1, tiled=True)  81.8 us
    reduce_scatter x1, waiting for transfers between devices, body(): lax.psum_scatter(part_kv, 'tensor', scatter_dimension=1, tiled=True)  76.3 us
    all_gather x1, blocking collectives, body(): lax.all_gather(positions, 'seq', axis=0, tiled=True)[None, :]  31.9 us
    psum x1, blocking collectives, body(): lax.psum((jnp.sum(slice_q * slice_q, axis=1), jnp.sum(slice_kv * slice_kv...  30.9 us
    all_gather x1, blocking collectives, body(): lax.all_gather(rope_key, 'seq', axis=0, tiled=True)  24 us
    all_gather x1, blocking collectives, body(): lax.all_gather(piece_q, 'tensor', axis=1, tiled=True)  20.5 us
    all_gather x1, blocking collectives, body(): lax.all_gather(piece_kv, 'tensor', axis=1, tiled=True)  15.6 us
    reshape x1, local copies, waits for them, and re-layouts, body(): keyval = keyval.reshape(count, HEAD_DEV, NOPE + VDIM)  14.5 us
  transfers between devices with their start and end apart: 4, of which 4 were waited for; matrix products, arithmetic and copies ran while one was open for 4% of the time, Pallas kernels for 0%

commit v1 on v0

v1 whole, which is shorter than its diff:
```python
import functools

import numpy as np
import jax
import jax.numpy as jnp
from jax import lax
from jax.experimental import pallas as pl
from jax.experimental.pallas import tpu as pltpu
from jax.sharding import PartitionSpec as P

NOPE = 128
ROPE = 64
VDIM = 128
HEAD_DEV = 4
QL = 1536
KVL = 512
WIDE = QL + KVL + 128
LINE = KVL + 128
RUN = 16
CHUNK = 512
MESH = pl.DeviceIdType.MESH
EPS = 1e-06
F32 = jnp.float32
BF16 = jnp.bfloat16

CUTS = (((0, 640), (640, 512)), ((1152, 512), (1664, 512)))


def turned(v, cosine, sine):
    lane = lax.broadcasted_iota(jnp.int32, v.shape, 1)
    swapped = jnp.where(lane < 32, -pltpu.roll(v, 96, 1), pltpu.roll(v, 32, 1))
    return jnp.where(lane < 64, v * cosine + swapped * sine, 0.0)


def kernel(
    pos_ref, freq_ref, gq_ref, gkv_ref, tok_hbm, wq_hbm, wkv_hbm, wr_hbm, uq_hbm, ukv_hbm,
    out_ref,
    tok, wq, wkv, wr, uq, ukv,
    part, l1x, l2x, l3x, r1x, r2x, r3x, l1y, l2y, l3y, r1y, r2y, r3y,
    mid_x, mid_y, k1x, k2x, k3x, j1x, j2x, j3x, k1y, k2y, k3y, j1y, j2y, j3y,
    total, lat_q, keys, qcat, m_ref, l_ref, acc_ref,
    load_sem, send_sem, recv_sem,
):
    s = lax.axis_index("seq")
    t = lax.axis_index("tensor")
    x, y = t // 4, t % 4
    z, c = s // 2, s % 2

    loads = []
    for n, (a, b) in enumerate(
        ((tok_hbm, tok), (wq_hbm, wq), (wkv_hbm, wkv), (wr_hbm, wr), (uq_hbm, uq), (ukv_hbm, ukv))
    ):
        loads.append(pltpu.make_async_copy(a, b, load_sem.at[n]))
        loads[-1].start()

    def at(xx, yy):
        return (s, xx * 4 + yy)

    xp, xm, xo = (x + 1) % 4, (x + 3) % 4, (x + 2) % 4
    yp, ym, yo = (y + 1) % 4, (y + 3) % 4, (y + 2) % 4
    x_plus, x_minus = at(xp, y), at(xm, y)
    y_plus, y_minus = at(x, yp), at(x, ym)
    sibling = (s + 1 - 2 * c, t)
    z_peers = [(((z + d) % 8) * 2 + c, t) for d in range(1, 8)]

    barrier = pltpu.get_barrier_semaphore()
    friends = [x_plus, x_minus, y_plus, y_minus, sibling] + z_peers
    for who in friends:
        pl.semaphore_signal(barrier, inc=1, device_id=who, device_id_type=MESH)

    sent = []
    count = [0]

    def fresh(n):
        count[0] += n
        return count[0] - n

    def send(src, dst, who, k):
        copy = pltpu.make_async_remote_copy(
            src_ref=src, dst_ref=dst, send_sem=send_sem.at[k], recv_sem=recv_sem.at[k],
            device_id=who, device_id_type=MESH,
        )
        copy.start()
        sent.append(copy)

    def arrived(dst, k):
        pltpu.make_async_remote_copy(
            src_ref=dst, dst_ref=dst, send_sem=send_sem.at[k], recv_sem=recv_sem.at[k],
            device_id=sibling, device_id_type=MESH,
        ).wait_recv()

    for n in range(4):
        loads[n].wait()
    tokens = tok[...]
    pq = jnp.dot(tokens, wq[...], preferred_element_type=F32)
    pkv = jnp.dot(tokens, wkv[...], preferred_element_type=F32)
    pr = jnp.dot(tokens, wr[...], preferred_element_type=F32)
    pr = jnp.concatenate([pr, jnp.zeros_like(pr)], axis=1)
    for i in range(16):
        rows = slice(i * RUN, (i + 1) * RUN)
        part[i // 4, i % 4, :, 0:QL] = pq[rows]
        part[i // 4, i % 4, :, QL : QL + KVL] = pkv[rows]
        part[i // 4, i % 4, :, QL + KVL : WIDE] = pr[rows]

    pl.semaphore_wait(barrier, len(friends))

    def ring_sum(ring, plus, minus, slab, bufs, base, done):
        me, nxt, prv, opp = ring
        L1, L2, L3, R1, R2, R3 = bufs
        send(slab(opp, 0), L1, plus, base)
        send(slab(opp, 1), R1, minus, base + 1)
        send(slab(nxt, 1), L2, plus, base + 2)
        send(slab(prv, 0), R2, minus, base + 3)
        yield
        arrived(L1, base)
        slab(nxt, 0)[...] = slab(nxt, 0)[...] + L1[...]
        send(slab(nxt, 0), L3, plus, base + 4)
        yield
        arrived(R1, base + 1)
        slab(prv, 1)[...] = slab(prv, 1)[...] + R1[...]
        send(slab(prv, 1), R3, minus, base + 5)
        yield
        for buf, k in ((L2, 2), (R2, 3), (L3, 4), (R3, 5)):
            arrived(buf, base + k)
        done(slab(me, 0)[...] + L3[...] + R2[...], slab(me, 1)[...] + L2[...] + R3[...])

    def color(n):
        (a0, aw), (b0, bw) = CUTS[n]
        first = (x, xp, xm, xo), x_plus, x_minus
        second = (y, yp, ym, yo), y_plus, y_minus
        if n == 1:
            first, second = second, first
        mid = mid_y if n else mid_x
        bufs1 = (l1y, l2y, l3y, r1y, r2y, r3y) if n else (l1x, l2x, l3x, r1x, r2x, r3x)
        bufs2 = (k1y, k2y, k3y, j1y, j2y, j3y) if n else (k1x, k2x, k3x, j1x, j2x, j3x)

        def slab1(i, half):
            cols = pl.ds(a0, aw) if half == 0 else pl.ds(b0, bw)
            return part.at[:, i, :, cols] if n else part.at[i, :, :, cols]

        def done1(a, b):
            mid[:, :, 0:aw] = a
            mid[:, :, aw : aw + bw] = b

        yield from ring_sum(*first, slab1, bufs1, fresh(6), done1)
        yield

        def slab2(i, half):
            return mid.at[i, :, pl.ds(0, aw)] if half == 0 else mid.at[i, :, pl.ds(aw, bw)]

        def done2(a, b):
            total[:, a0 : a0 + aw] = a
            total[:, b0 : b0 + bw] = b

        yield from ring_sum(*second, slab2, bufs2, fresh(6), done2)

    def run(tasks):
        tasks = list(tasks)
        while tasks:
            for task in list(tasks):
                try:
                    next(task)
                except StopIteration:
                    tasks.remove(task)

    run([color(0), color(1)])

    def normed(v, gain, width):
        mean_sq = jnp.sum(v * v, axis=1, keepdims=True) / width
        return (v * lax.rsqrt(mean_sq + EPS) * gain).astype(BF16)

    at_run = pos_ref[t * RUN]
    where_at = at_run + lax.broadcasted_iota(jnp.int32, (RUN, 128), 0)
    angle = where_at.astype(F32) * freq_ref[...]
    key = turned(total[:, QL + KVL : WIDE], jnp.cos(angle), jnp.sin(angle))
    lane = lax.broadcasted_iota(jnp.int32, (RUN, 128), 1)
    high = (where_at >> 6).astype(F32)
    low = (where_at & 63).astype(F32)
    key = jnp.where(lane == 64, high, jnp.where(lane == 65, low, key)).astype(BF16)

    def spot(zz):
        hue = zz // 4
        return hue, (1 - hue) * (x * 4 + y) + hue * (y * 4 + x), zz % 4

    hue, place, zrow = spot(z)
    keys[hue, place, c, zrow, :, 0:KVL] = normed(total[:, QL : QL + KVL], gkv_ref[...], KVL)
    keys[hue, place, c, zrow, :, KVL:LINE] = key
    lat_q[t] = normed(total[:, 0:QL], gq_ref[...], QL)

    zbase = fresh(7)
    mine = keys.at[hue, place, c, zrow]
    for d in range(1, 8):
        send(mine, mine, z_peers[d - 1], zbase + d - 1)

    def ring_gather(ring, plus, minus, unit, half, base, got):
        me, nxt, prv, opp = ring
        send(unit(me), unit(me), plus, base)
        send(unit(me), unit(me), minus, base + 1)
        got(me)
        yield
        arrived(unit(prv), base)
        send(half(prv, 0), half(prv, 0), plus, base + 2)
        got(prv)
        yield
        arrived(unit(nxt), base + 1)
        send(half(nxt, 1), half(nxt, 1), minus, base + 3)
        got(nxt)
        yield
        arrived(half(opp, 0), base + 2)
        arrived(half(opp, 1), base + 3)
        got(opp)

    def plane_gather(n, unit, half, tasks, got):
        first = (x, xp, xm, xo), x_plus, x_minus
        second = (y, yp, ym, yo), y_plus, y_minus
        if n == 1:
            first, second = second, first
        other = second[0][0]

        def got1(i):
            def unit2(j):
                return unit(i, j)

            def half2(j, h):
                return half(i, j, h)

            tasks.append(ring_gather(*second, unit2, half2, fresh(4), lambda j: got(i, j)))

        return ring_gather(*first, lambda i: unit(i, other), lambda i, h: half(i, other, h), fresh(4), got1)

    def run_growing(tasks):
        while tasks:
            for task in list(tasks):
                try:
                    next(task)
                except StopIteration:
                    tasks.remove(task)

    tasks = []
    for n in range(2):
        def q_unit(i, j, n=n):
            return lat_q.at[(j * 4 + i) if n else (i * 4 + j), :, pl.ds(768 * n, 768)]

        def q_half(i, j, h, n=n):
            return lat_q.at[(j * 4 + i) if n else (i * 4 + j), :, pl.ds(768 * n + 384 * h, 384)]

        tasks.append(plane_gather(n, q_unit, q_half, tasks, lambda i, j: None))
    run_growing(tasks)

    for d in range(1, 8):
        h2, p2, r2 = spot((z + 8 - d) % 8)
        arrived(keys.at[h2, p2, c, r2], zbase + d - 1)

    tasks = []
    pairs = []
    for n in range(2):
        def k_unit(i, j, n=n):
            return keys.at[n, i * 4 + j, c]

        def k_half(i, j, h, n=n):
            return keys.at[n, i * 4 + j, c, pl.ds(2 * h, 2)]

        def k_got(i, j, n=n):
            k = fresh(1)
            send(keys.at[n, i * 4 + j, c], keys.at[n, i * 4 + j, c], sibling, k)
            pairs.append((keys.at[n, i * 4 + j, 1 - c], k))

        tasks.append(plane_gather(n, k_unit, k_half, tasks, k_got))
    run_growing(tasks)
    for ref, k in pairs:
        arrived(ref, k)

    loads[4].wait()
    loads[5].wait()
    query = jnp.dot(lat_q[...].reshape(16 * RUN, QL), uq[...], preferred_element_type=F32)
    qpos = jnp.concatenate(
        [pos_ref[i * RUN] + lax.broadcasted_iota(jnp.int32, (RUN, 128), 0) for i in range(16)], axis=0
    ).astype(F32)
    qangle = qpos * freq_ref[...]
    qcos, qsin = jnp.cos(qangle), jnp.sin(qangle)
    for h in range(HEAD_DEV):
        qcat[h, :, 0:128] = query[:, 192 * h : 192 * h + 128].astype(BF16)
        tail = query[:, 192 * h + 128 : 192 * h + 192]
        tail = jnp.concatenate([tail, jnp.zeros_like(tail)], axis=1)
        qcat[h, :, 128:256] = turned(tail, qcos, qsin).astype(BF16)
    m_ref[...] = jnp.full_like(m_ref, -1e30)
    l_ref[...] = jnp.zeros_like(l_ref)
    acc_ref[...] = jnp.zeros_like(acc_ref)
    scale = np.float32((1.0 + 0.1 * np.log(40.0)) ** 2 / np.sqrt(192.0))
    qcol = qpos[:, 0:1]
    lane8 = lax.broadcasted_iota(jnp.int32, (8, 128), 1)
    pick = jnp.where(lane8 == 64, 64.0, jnp.where(lane8 == 65, 1.0, 0.0)).astype(BF16)

    def chunk(n, o):
        rows = keys[n, pl.ds(o * 4, 4)].reshape(CHUNK, LINE)
        rope_rows = rows[:, KVL:LINE]
        up = jnp.dot(rows[:, 0:KVL], ukv[...], preferred_element_type=F32).astype(BF16)
        kpos = lax.dot_general(pick, rope_rows, (((1,), (1,)), ((), ())), preferred_element_type=F32)[0:1]
        seen = kpos <= qcol
        for h in range(HEAD_DEV):
            kcat = jnp.concatenate([up[:, 256 * h : 256 * h + 128], rope_rows], axis=1)
            sc = lax.dot_general(qcat[h], kcat, (((1,), (1,)), ((), ())), preferred_element_type=F32)
            sc = jnp.where(seen, sc * scale, -1e30)
            old = m_ref[h]
            new = jnp.maximum(old, jnp.max(sc, axis=1, keepdims=True))
            fade = jnp.exp(old - new)
            w = jnp.exp(sc - new)
            m_ref[h] = new
            l_ref[h] = l_ref[h] * fade + jnp.sum(w, axis=1, keepdims=True)
            acc_ref[h] = acc_ref[h] * fade + jnp.dot(
                w.astype(BF16), up[:, 256 * h + 128 : 256 * h + 256], preferred_element_type=F32
            )

    def step(i, _):
        chunk(i // 4, i % 4)
        return 0

    lax.fori_loop(0, 8, step, 0)
    for h in range(HEAD_DEV):
        out_ref[:, VDIM * h : VDIM * (h + 1)] = (acc_ref[h] / l_ref[h]).astype(BF16)

    for copy in sent:
        copy.wait_send()
    assert count[0] <= SEMS, count[0]


SEMS = 160
FREQ = np.zeros((1, 128), np.float32)
FREQ[0, :64] = np.tile(
    np.float32(10000.0) ** (-(np.arange(32, dtype=np.float32) * np.float32(2.0) / np.float32(64))), 2
)


def body(tokens, positions, w_down_q, w_down_kv, w_rope_key, gain_query, gain_kv, w_up_q, w_up_kv):
    vmem = pl.BlockSpec(memory_space=pltpu.VMEM)
    smem = pl.BlockSpec(memory_space=pltpu.SMEM)
    any_ = pl.BlockSpec(memory_space=pl.ANY)

    def sums(lead, n):
        (_, aw), (_, bw) = CUTS[n]
        return [pltpu.VMEM(lead + (w,), F32) for w in (aw, bw, aw, bw, aw, bw)]

    scratch = (
        [pltpu.VMEM(a.shape, a.dtype) for a in (tokens, w_down_q, w_down_kv, w_rope_key, w_up_q, w_up_kv)]
        + [pltpu.VMEM((4, 4, RUN, WIDE), F32)]
        + sums((4, RUN), 0)
        + sums((4, RUN), 1)
        + [pltpu.VMEM((4, RUN, 1152), F32), pltpu.VMEM((4, RUN, 1024), F32)]
        + sums((RUN,), 0)
        + sums((RUN,), 1)
        + [
            pltpu.VMEM((RUN, WIDE), F32),
            pltpu.VMEM((16, RUN, QL), BF16),
            pltpu.VMEM((2, 16, 2, 4, RUN, LINE), BF16),
            pltpu.VMEM((HEAD_DEV, 256, 256), BF16),
            pltpu.VMEM((HEAD_DEV, 256, 1), F32),
            pltpu.VMEM((HEAD_DEV, 256, 1), F32),
            pltpu.VMEM((HEAD_DEV, 256, VDIM), F32),
            pltpu.SemaphoreType.DMA((6,)),
            pltpu.SemaphoreType.DMA((SEMS,)),
            pltpu.SemaphoreType.DMA((SEMS,)),
        ]
    )
    return pl.pallas_call(
        kernel,
        out_shape=jax.ShapeDtypeStruct((256, HEAD_DEV * VDIM), BF16),
        in_specs=[smem, vmem, vmem, vmem] + [any_] * 6,
        out_specs=vmem,
        scratch_shapes=scratch,
        compiler_params=pltpu.CompilerParams(
            collective_id=0, has_side_effects=True, vmem_limit_bytes=56 * 1024 * 1024
        ),
    )(
        positions, jnp.asarray(FREQ), gain_query.reshape(1, QL), gain_kv.reshape(1, KVL),
        tokens, w_down_q, w_down_kv, w_rope_key, w_up_q, w_up_kv,
    )


def solution(mesh):
    in_specs = (
        P("seq", "tensor"),
        P("seq"),
        P("tensor", None),
        P("tensor", None),
        P("tensor", None),
        P(),
        P(),
        P(None, "tensor"),
        P(None, "tensor"),
    )
    out_specs = P("seq", "tensor")
    return jax.shard_map(body, mesh=mesh, in_specs=in_specs, out_specs=out_specs, check_vma=False)
```

time: 399 us -> 108 us (0.27)
  waiting for transfers between devices: 179 us -> 0 us
  blocking collectives: 123 us -> 0 us
  Pallas kernels: 0 us -> 102 us
  matrix products: 41.4 us -> 0 us
  local copies, waits for them, and re-layouts: 25.9 us -> 6.34 us
  other arithmetic: 15.2 us -> 0 us
  between operations: 13.2 us -> 0.01 us
    reduce_scatter x2 -> x0, waiting for transfers between devices: 158 us -> none  [the longest x1 81.8 us: body(): lax.psum_scatter(part_q, 'tensor', scatter_dimension=1, tiled=True)]
    pallas_call x0 -> x1, Pallas kernels: none -> 102 us  [body(): pl.pallas_call(kernel, out_shape=jax.ShapeDtypeStruct((256, HEAD_DEV * VD...]
    all_gather x4 -> x0, blocking collectives: 92.1 us -> none  [the longest x1 31.9 us: body(): lax.all_gather(positions, 'seq', axis=0, tiled=True)[None, :]]
    dot_general x8 -> x0, matrix products: 41.4 us -> none  [the longest x1 11.2 us: body(): jnp.einsum('qhk,khd->qhd', weights.astype(jnp.bfloat16), values, preferre...]
    psum x1 -> x0, blocking collectives: 30.9 us -> none  [body(): lax.psum((jnp.sum(slice_q * slice_q, axis=1), jnp.sum(slice_kv * slice_kv...]
    reshape x2 -> x1, local copies, waits for them, and re-layouts: 16.3 us -> 1.29 us  [body(): gain_query.reshape(1, QL)]
    all_gather x1 -> x0, waiting for transfers between devices: 11.4 us -> none  [body(): keyval = lax.all_gather(keyval_local, 'seq', axis=0, tiled=True)]
    reduce_sum x3 -> x0, other arithmetic: 10.5 us -> none  [the longest x1 8.75 us: body(): total = total * factor + jnp.sum(weights, axis=-1)]
  transfers between devices with their start and end apart: 4 -> 0, of which waited for: 4 -> 0; matrix products, arithmetic and copies ran while one was open for 4% -> 0% of each run, Pallas kernels for 0% -> 0%
where the time goes in v1:
time: 108 us
  Pallas kernels  102 us (94%)
  local copies, waits for them, and re-layouts  6.34 us (6%)
    pallas_call x1, Pallas kernels, body(): pl.pallas_call(kernel, out_shape=jax.ShapeDtypeStruct((256, HEAD_DEV * VD...  102 us
    unnamed x3, local copies, waits for them, and re-layouts  5.05 us

profile of v1, /device:TPU:1, one launch (start us, length us, event | category | flops | bytes accessed | tf_op | source)
XLA Modules:
  0.0 108.1 jit_solution(1127243506381760215)
XLA Ops:
  0.0 1.3 %reshape.6.gq_ref = f32[1,1536]{1,0:T(1,128)} reshape(f32[1536]{0:T(1024)} %param.15) | data formatting | bytes 12288 | tf_op jit(solution)/shard_map/reshape | solution.py:374
  1.3 1.6 %copy.12.wr_hbm = bf16[448,64]{1,0:T(8,128)(2,1)} copy(bf16[448,64]{0,1:T(8,128)(2,1)} %param.14) | data formatting | bytes 114688 | tf_op args[4]
  2.9 1.8 %copy.11.tok_hbm = bf16[256,448]{1,0:T(8,128)(2,1)} copy(bf16[256,448]{0,1:T(8,128)(2,1)} %param.10) | data formatting | bytes 458752 | tf_op args[0]
  4.7 101.7 %shard_map.100 = bf16[256,512]{1,0:T(8,128)(2,1)} custom-call(s32[256]{0:T(256)} %pos_ref.1, f32[1,128]{1,0:T(1,128)} %constant.2.clone.freq_ref, f32[1,1536]{1,0:T(1,128)} %reshape.6.gq_ref, f32[1,512]{1,0:T(1,128)} %bitcast.1, bf16[256,448]{1,0:T(8,128)(2,1)} %copy.11.tok_hbm, bf16[448,1536]{1,0:T(8,128)(2,1)} %wq_hbm.1, bf16[448,512]{1,0:T(8,128)(2,1)} %wkv_hbm.1, ...), custom_call_target="tpu_custom_call" | custom-call | tf_op jit(solution)/shard_map/pallas_call | solution.py:364
  106.4 1.7 %copy.14 = bf16[256,512]{1,0:T(8,128)(2,1)} copy(bf16[256,512]{1,0:T(8,128)(2,1)} %shard_map.100) | data formatting | bytes 524288

commit v2 on v1

v2 whole, which is shorter than its diff:
```python
import functools

import numpy as np
import jax
import jax.numpy as jnp
from jax import lax
from jax.experimental import pallas as pl
from jax.experimental.pallas import tpu as pltpu
from jax.sharding import PartitionSpec as P

NOPE = 128
ROPE = 64
VDIM = 128
HEAD_DEV = 4
QL = 1536
KVL = 512
LINE = KVL + 128
RUN = 16
GROUP = 512
MESH = pl.DeviceIdType.MESH
EPS = 1e-06
F32 = jnp.float32
BF16 = jnp.bfloat16

CUTS_Q = (((0, 384), (384, 384)), ((768, 384), (1152, 384)))
CUTS_K = (((0, 128), (128, 128)), ((256, 256), (512, 128)))


def turned(v, cosine, sine):
    lane = lax.broadcasted_iota(jnp.int32, v.shape, 1)
    swapped = jnp.where(lane < 32, -pltpu.roll(v, 96, 1), pltpu.roll(v, 32, 1))
    return jnp.where(lane < 64, v * cosine + swapped * sine, 0.0)


def kernel(
    pos_ref, freq_ref, gq_ref, gkv_ref, tok_hbm, wq_hbm, wkv_hbm, wr_hbm, uq_hbm, ukv_hbm,
    out_ref,
    tok, wq, wkv, wr, uq, ukv,
    part_q, part_k, bufs_q, bufs_k, mids_q, mids_k, small_q, small_k,
    total_q, total_k, lat_q, keys, up_ref, rope_ref, qcat, m_ref, l_ref, acc_ref,
    load_sem, send_sem, recv_sem,
):
    s = lax.axis_index("seq")
    t = lax.axis_index("tensor")
    x, y = t // 4, t % 4
    z, c = s // 2, s % 2

    loads = []
    for n, (a, b) in enumerate(
        ((tok_hbm, tok), (wkv_hbm, wkv), (wr_hbm, wr), (wq_hbm, wq), (uq_hbm, uq), (ukv_hbm, ukv))
    ):
        loads.append(pltpu.make_async_copy(a, b, load_sem.at[n]))
        loads[-1].start()

    def at(xx, yy):
        return (s, xx * 4 + yy)

    ring_x = (x, (x + 1) % 4, (x + 3) % 4, (x + 2) % 4)
    ring_y = (y, (y + 1) % 4, (y + 3) % 4, (y + 2) % 4)
    along_x = ring_x, at(ring_x[1], y), at(ring_x[2], y)
    along_y = ring_y, at(x, ring_y[1]), at(x, ring_y[2])
    sibling = (s + 1 - 2 * c, t)
    z_peers = [(((z + d) % 8) * 2 + c, t) for d in range(1, 8)]

    barrier = pltpu.get_barrier_semaphore()
    friends = [*along_x[1:], *along_y[1:], sibling] + z_peers
    for who in friends:
        pl.semaphore_signal(barrier, inc=1, device_id=who, device_id_type=MESH)

    sent = []
    count = [0]

    def fresh(n):
        count[0] += n
        return count[0] - n

    def send(src, dst, who, k):
        copy = pltpu.make_async_remote_copy(
            src_ref=src, dst_ref=dst, send_sem=send_sem.at[k], recv_sem=recv_sem.at[k],
            device_id=who, device_id_type=MESH,
        )
        copy.start()
        sent.append(copy)

    def arrived(dst, k):
        pltpu.make_async_remote_copy(
            src_ref=dst, dst_ref=dst, send_sem=send_sem.at[k], recv_sem=recv_sem.at[k],
            device_id=sibling, device_id_type=MESH,
        ).wait_recv()

    def ring_sum(along, slab, bufs, done, split):
        (me, nxt, prv, opp), plus, minus = along
        L1, L2, L3, R1, R2, R3 = bufs
        base = fresh(6)
        send(slab(opp, 0), L1, plus, base)
        send(slab(opp, 1), R1, minus, base + 1)
        if split:
            yield
        send(slab(nxt, 1), L2, plus, base + 2)
        send(slab(prv, 0), R2, minus, base + 3)
        yield
        arrived(L1, base)
        slab(nxt, 0)[...] = slab(nxt, 0)[...] + L1[...]
        send(slab(nxt, 0), L3, plus, base + 4)
        arrived(R1, base + 1)
        slab(prv, 1)[...] = slab(prv, 1)[...] + R1[...]
        send(slab(prv, 1), R3, minus, base + 5)
        yield
        for buf, k in ((L2, 2), (R2, 3), (L3, 4), (R3, 5)):
            arrived(buf, base + k)
        done(slab(me, 0)[...] + L3[...] + R2[...], slab(me, 1)[...] + L2[...] + R3[...])

    def summed(n, cuts, part, bufs, mid, small, total, split):
        (a0, aw), (b0, bw) = cuts[n]
        first, second = (along_y, along_x) if n else (along_x, along_y)

        def slab1(i, half):
            cols = pl.ds(b0, bw) if half else pl.ds(a0, aw)
            return part.at[:, i, :, cols] if n else part.at[i, :, :, cols]

        def slab2(i, half):
            return mid.at[i, :, pl.ds(aw, bw) if half else pl.ds(0, aw)]

        def done1(a, b):
            mid[:, :, 0:aw] = a
            mid[:, :, aw : aw + bw] = b

        def done2(a, b):
            total[:, a0 : a0 + aw] = a
            total[:, b0 : b0 + bw] = b

        yield from ring_sum(first, slab1, bufs, done1, split)
        yield from ring_sum(second, slab2, small, done2, False)

    sum_k = [summed(n, CUTS_K, part_k, bufs_k[n], mids_k[n], small_k[n], total_k, False) for n in range(2)]
    sum_q = [summed(n, CUTS_Q, part_q, bufs_q[n], mids_q[n], small_q[n], total_q, True) for n in range(2)]

    def go(tasks):
        for task in tasks:
            next(task, None)

    loads[0].wait()
    loads[1].wait()
    loads[2].wait()
    tokens = tok[...].T
    pk = jnp.dot(tokens, wkv[...], preferred_element_type=F32)
    pr = lax.dot_general(tokens, wr[...], (((1,), (1,)), ((), ())), preferred_element_type=F32)
    pr = jnp.concatenate([pr, jnp.zeros_like(pr)], axis=1)
    for i in range(16):
        rows = slice(i * RUN, (i + 1) * RUN)
        part_k[i // 4, i % 4, :, 0:KVL] = pk[rows]
        part_k[i // 4, i % 4, :, KVL:LINE] = pr[rows]
    pl.semaphore_wait(barrier, len(friends))
    go(sum_k)

    loads[3].wait()
    pq = jnp.dot(tokens, wq[...], preferred_element_type=F32)
    for i in range(16):
        part_q[i // 4, i % 4] = pq[i * RUN : (i + 1) * RUN]
    go(sum_q)
    go(sum_k)
    go(sum_q)
    go(sum_k)
    go(sum_q)
    go(sum_k)
    go(sum_q)

    def normed(v, gain, width):
        mean_sq = jnp.sum(v * v, axis=1, keepdims=True) / width
        return (v * lax.rsqrt(mean_sq + EPS) * gain).astype(BF16)

    at_run = pos_ref[t * RUN]
    where_at = at_run + lax.broadcasted_iota(jnp.int32, (RUN, 128), 0)
    angle = where_at.astype(F32) * freq_ref[...]
    cosine, sine = jnp.cos(angle), jnp.sin(angle)
    lane = lax.broadcasted_iota(jnp.int32, (RUN, 128), 1)
    high = (where_at >> 6).astype(F32)
    low = (where_at & 63).astype(F32)

    go(sum_k)
    key = turned(total_k[:, KVL:LINE], cosine, sine)
    key = jnp.where(lane == 64, high, jnp.where(lane == 65, low, key)).astype(BF16)

    def spot(zz):
        hue = zz // 4
        return hue, (1 - hue) * (x * 4 + y) + hue * (y * 4 + x), zz % 4

    hue, place, zrow = spot(z)
    keys[hue, place, c, zrow, :, 0:KVL] = normed(total_k[:, 0:KVL], gkv_ref[...], KVL)
    keys[hue, place, c, zrow, :, KVL:LINE] = key

    zbase = fresh(7)
    mine = keys.at[hue, place, c, zrow]
    for d in range(1, 8):
        send(mine, mine, z_peers[d - 1], zbase + d - 1)

    class Gather:
        def __init__(self, n, unit, half, got):
            self.first, self.second = (along_y, along_x) if n else (along_x, along_y)
            self.unit, self.half, self.got = unit, half, got
            self.base1 = fresh(4)
            self.base2 = [fresh(4) for _ in range(4)]

        def name(self, i, j):
            return self.first[0][i], self.second[0][j]

        def start2(self, i):
            u = self.unit(*self.name(i, 0))
            send(u, u, self.second[1], self.base2[i])
            send(u, u, self.second[2], self.base2[i] + 1)
            self.got(*self.name(i, 0))

        def start(self):
            u = self.unit(*self.name(0, 0))
            send(u, u, self.first[1], self.base1)
            send(u, u, self.first[2], self.base1 + 1)
            self.start2(0)

        def take(self, where, pick, base, along):
            if pick == 3:
                arrived(self.half(*where, 0), base + 2)
                arrived(self.half(*where, 1), base + 3)
            elif pick == 2:
                arrived(self.unit(*where), base)
                h = self.half(*where, 0)
                send(h, h, along[1], base + 2)
            else:
                arrived(self.unit(*where), base + 1)
                h = self.half(*where, 1)
                send(h, h, along[2], base + 3)

        def arrive1(self, i):
            self.take(self.name(i, 0), i, self.base1, self.first)
            self.start2(i)

        def arrive2(self, i, j):
            self.take(self.name(i, j), j, self.base2[i], self.second)
            self.got(*self.name(i, j))

    pairs = {}

    def gather_q(n):
        def unit(i, j):
            return lat_q.at[(j * 4 + i) if n else (i * 4 + j), :, pl.ds(768 * n, 768)]

        def half(i, j, h):
            return lat_q.at[(j * 4 + i) if n else (i * 4 + j), :, pl.ds(768 * n + 384 * h, 384)]

        return Gather(n, unit, half, lambda i, j: None)

    def gather_k(n):
        def unit(i, j):
            return keys.at[n, i * 4 + j, c]

        def half(i, j, h):
            return keys.at[n, i * 4 + j, c, pl.ds(2 * h, 2)]

        def got(i, j):
            k = fresh(1)
            send(unit(i, j), unit(i, j), sibling, k)
            pairs.setdefault(n, []).append((keys.at[n, i * 4 + j, 1 - c], k))

        return Gather(n, unit, half, got)

    go(sum_q)
    go(sum_q)
    gain_q = jnp.concatenate([gq_ref[i : i + 1, :] for i in range(QL // 128)], axis=1)
    lat_q[t] = normed(total_q[...], gain_q, QL)

    gq = [gather_q(n) for n in range(2)]
    gk = [gather_k(n) for n in range(2)]
    for g in gq:
        g.start()
    for d in range(1, 8):
        h2, p2, r2 = spot((z + 8 - d) % 8)
        arrived(keys.at[h2, p2, c, r2], zbase + d - 1)
    for g in gk:
        g.start()

    scale = np.float32((1.0 + 0.1 * np.log(40.0)) ** 2 / np.sqrt(192.0))
    lane8 = lax.broadcasted_iota(jnp.int32, (8, 128), 1)
    pick = jnp.where(lane8 == 64, 64.0, jnp.where(lane8 == 65, 1.0, 0.0)).astype(BF16)
    m_ref[...] = jnp.full_like(m_ref, -1e30)
    l_ref[...] = jnp.zeros_like(l_ref)
    acc_ref[...] = jnp.zeros_like(acc_ref)
    qpos = jnp.concatenate(
        [pos_ref[i * RUN] + lax.broadcasted_iota(jnp.int32, (RUN, 128), 0) for i in range(16)], axis=0
    ).astype(F32)
    qcol = qpos[:, 0:1]

    def queries():
        query = jnp.dot(lat_q[...].reshape(16 * RUN, QL), uq[...], preferred_element_type=F32)
        qangle = qpos * freq_ref[...]
        qcos, qsin = jnp.cos(qangle), jnp.sin(qangle)
        for h in range(HEAD_DEV):
            qcat[h, :, 0:128] = query[:, 192 * h : 192 * h + 128].astype(BF16)
            tail = query[:, 192 * h + 128 : 192 * h + 192]
            tail = jnp.concatenate([tail, jnp.zeros_like(tail)], axis=1)
            qcat[h, :, 128:256] = turned(tail, qcos, qsin).astype(BF16)

    groups = (
        ((0, 0), (2, 0)), ((1, 0), (0, 2)), ((0, 1), (3, 0)), ((2, 2), (2, 1)),
        ((1, 2), (1, 1)), ((0, 3), (3, 2)), ((3, 1), (2, 3)), ((1, 3), (3, 3)),
    )
    def expand(g):
        rows = []
        for n in range(2):
            for i, j in groups[g]:
                p, q = gk[n].name(i, j)
                ref, k = pairs[n][sequence.index((i, j))]
                arrived(ref, k)
                rows.append(keys[n, p * 4 + q].reshape(128, LINE))
        rows = jnp.concatenate(rows, axis=0)
        rope_ref[g] = rows[:, KVL:LINE]
        up_ref[g] = jnp.dot(rows[:, 0:KVL], ukv[...], preferred_element_type=F32).astype(BF16)

    def attend(g):
        rope_rows = rope_ref[g]
        kpos = lax.dot_general(pick, rope_rows, (((1,), (1,)), ((), ())), preferred_element_type=F32)[0:1]
        seen = kpos <= qcol
        for h in range(HEAD_DEV):
            kcat = jnp.concatenate([up_ref[g, :, 256 * h : 256 * h + 128], rope_rows], axis=1)
            sc = lax.dot_general(qcat[h], kcat, (((1,), (1,)), ((), ())), preferred_element_type=F32)
            sc = jnp.where(seen, sc * scale, -1e30)
            old = m_ref[h]
            new = jnp.maximum(old, jnp.max(sc, axis=1, keepdims=True))
            fade = jnp.exp(old - new)
            w = jnp.exp(sc - new)
            m_ref[h] = new
            l_ref[h] = l_ref[h] * fade + jnp.sum(w, axis=1, keepdims=True)
            acc_ref[h] = acc_ref[h] * fade + jnp.dot(
                w.astype(BF16), up_ref[g, :, 256 * h + 128 : 256 * h + 256], preferred_element_type=F32
            )

    sequence = [(0, 0)]

    def k_step(*steps):
        for step in steps:
            for g in gk:
                if isinstance(step, int):
                    g.arrive1(step)
                else:
                    g.arrive2(*step)
            sequence.append((step, 0) if isinstance(step, int) else step)

    def q_step(*steps):
        for step in steps:
            for g in gq:
                if isinstance(step, int):
                    g.arrive1(step)
                else:
                    g.arrive2(*step)

    q_step(2, 1)
    q_step((0, 2), (0, 1))
    k_step(2, 1)
    q_step(3)
    k_step((0, 2), (0, 1), 3)
    q_step((2, 2), (2, 1), (1, 2), (1, 1), (0, 3))
    loads[5].wait()
    expand(0)
    k_step((2, 2), (2, 1), (1, 2), (1, 1))
    q_step((3, 2), (3, 1), (2, 3), (1, 3))
    expand(1)
    k_step((0, 3), (3, 2), (3, 1))
    q_step((3, 3))
    loads[4].wait()
    queries()
    attend(0)
    expand(2)
    attend(1)
    k_step((2, 3), (1, 3), (3, 3))
    attend(2)
    for g in range(3, 8):
        expand(g)
        attend(g)
    for h in range(HEAD_DEV):
        out_ref[:, VDIM * h : VDIM * (h + 1)] = (acc_ref[h] / l_ref[h]).astype(BF16)

    for copy in sent:
        copy.wait_send()
    assert count[0] <= SEMS, count[0]


SEMS = 176
FREQ = np.zeros((1, 128), np.float32)
FREQ[0, :64] = np.tile(
    np.float32(10000.0) ** (-(np.arange(32, dtype=np.float32) * np.float32(2.0) / np.float32(64))), 2
)


def body(tokens, positions, w_down_q, w_down_kv, w_rope_key, gain_query, gain_kv, w_up_q, w_up_kv):
    vmem = pl.BlockSpec(memory_space=pltpu.VMEM)
    smem = pl.BlockSpec(memory_space=pltpu.SMEM)
    any_ = pl.BlockSpec(memory_space=pl.ANY)

    def sums(lead, cuts):
        out = []
        for (_, aw), (_, bw) in cuts:
            out.append([pltpu.VMEM(lead + (w,), F32) for w in (aw, bw, aw, bw, aw, bw)])
        return out

    def mids(cuts):
        return [pltpu.VMEM((4, RUN, a[1] + b[1]), F32) for a, b in cuts]

    tokens, w_rope_key = tokens.T, w_rope_key.T
    scratch = (
        [pltpu.VMEM(a.shape, a.dtype) for a in (tokens, w_down_q, w_down_kv, w_rope_key, w_up_q, w_up_kv)]
        + [pltpu.VMEM((4, 4, RUN, QL), F32), pltpu.VMEM((4, 4, RUN, LINE), F32)]
        + [sums((4, RUN), CUTS_Q), sums((4, RUN), CUTS_K), mids(CUTS_Q), mids(CUTS_K)]
        + [sums((RUN,), CUTS_Q), sums((RUN,), CUTS_K)]
        + [
            pltpu.VMEM((RUN, QL), F32),
            pltpu.VMEM((RUN, LINE), F32),
            pltpu.VMEM((16, RUN, QL), BF16),
            pltpu.VMEM((2, 16, 2, 4, RUN, LINE), BF16),
            pltpu.VMEM((8, GROUP, 1024), BF16),
            pltpu.VMEM((8, GROUP, 128), BF16),
            pltpu.VMEM((HEAD_DEV, 256, 256), BF16),
            pltpu.VMEM((HEAD_DEV, 256, 1), F32),
            pltpu.VMEM((HEAD_DEV, 256, 1), F32),
            pltpu.VMEM((HEAD_DEV, 256, VDIM), F32),
            pltpu.SemaphoreType.DMA((6,)),
            pltpu.SemaphoreType.DMA((SEMS,)),
            pltpu.SemaphoreType.DMA((SEMS,)),
        ]
    )
    return pl.pallas_call(
        kernel,
        out_shape=jax.ShapeDtypeStruct((256, HEAD_DEV * VDIM), BF16),
        in_specs=[smem, vmem, vmem, vmem] + [any_] * 6,
        out_specs=vmem,
        scratch_shapes=scratch,
        compiler_params=pltpu.CompilerParams(
            collective_id=0, has_side_effects=True, vmem_limit_bytes=56 * 1024 * 1024
        ),
    )(
        positions, jnp.asarray(FREQ), gain_query.reshape(QL // 128, 128), gain_kv.reshape(1, KVL),
        tokens, w_down_q, w_down_kv, w_rope_key, w_up_q, w_up_kv,
    )


def solution(mesh):
    in_specs = (
        P("seq", "tensor"),
        P("seq"),
        P("tensor", None),
        P("tensor", None),
        P("tensor", None),
        P(),
        P(),
        P(None, "tensor"),
        P(None, "tensor"),
    )
    out_specs = P("seq", "tensor")
    return jax.shard_map(body, mesh=mesh, in_specs=in_specs, out_specs=out_specs, check_vma=False)
```

time: 108 us -> 73.8 us (0.68)
  the two profiles are of different devices: /device:TPU:1 before, /device:TPU:6 now
where the time goes in v2:
time: 73.8 us; the launch traced here: 73.7 us
  Pallas kernels  72 us (98%)
  local copies, waits for them, and re-layouts  1.67 us (2%)
    pallas_call x1, Pallas kernels, body(): pl.pallas_call(kernel, out_shape=jax.ShapeDtypeStruct((256, HEAD_DEV * VD...  72 us
    unnamed x1, local copies, waits for them, and re-layouts  1.67 us

profile of v2, /device:TPU:6, one launch (start us, length us, event | category | flops | bytes accessed | tf_op | source)
XLA Modules:
  0.0 73.7 jit_solution(6687601472496782632)
XLA Ops:
  0.0 72.0 %shard_map.100 = bf16[256,512]{1,0:T(8,128)(2,1)} custom-call(s32[256]{0:T(256)} %pos_ref.1, f32[1,128]{1,0:T(1,128)} %constant.2.clone.freq_ref, f32[12,128]{1,0:T(8,128)} %bitcast.6, f32[1,512]{1,0:T(1,128)} %bitcast.7, bf16[448,256]{1,0:T(8,128)(2,1)} %bitcast.4, bf16[448,1536]{1,0:T(8,128)(2,1)} %wq_hbm.1, bf16[448,512]{1,0:T(8,128)(2,1)} %wkv_hbm.1, ...), custom_call_target="tpu_custom_call" | custom-call | tf_op jit(solution)/shard_map/pallas_call | solution.py:428
  72.0 1.7 %copy.12 = bf16[256,512]{1,0:T(8,128)(2,1)} copy(bf16[256,512]{1,0:T(8,128)(2,1)} %shard_map.100) | data formatting | bytes 524288

commit v3 on v2

--- a/solution.py
+++ b/solution.py
@@ -33,12 +33,12 @@
 
 
 def kernel(
-    pos_ref, freq_ref, gq_ref, gkv_ref, tok_hbm, wq_hbm, wkv_hbm, wr_hbm, uq_hbm, ukv_hbm,
+    pos_ref, freq_hbm, gq_hbm, gkv_hbm, tok_hbm, wq_hbm, wkv_hbm, wr_hbm, uq_hbm, ukv_hbm,
     out_ref,
-    tok, wq, wkv, wr, uq, ukv,
+    tok, wq, wkv, wr, uq, ukv, freq_ref, gq_ref, gkv_ref,
     part_q, part_k, bufs_q, bufs_k, mids_q, mids_k, small_q, small_k,
     total_q, total_k, lat_q, keys, up_ref, rope_ref, qcat, m_ref, l_ref, acc_ref,
-    load_sem, send_sem, recv_sem,
+    load_sem, send_sem, recv_sem, near_sem,
 ):
     s = lax.axis_index("seq")
     t = lax.axis_index("tensor")
@@ -47,7 +47,10 @@
 
     loads = []
     for n, (a, b) in enumerate(
-        ((tok_hbm, tok), (wkv_hbm, wkv), (wr_hbm, wr), (wq_hbm, wq), (uq_hbm, uq), (ukv_hbm, ukv))
+        (
+            (tok_hbm, tok), (wkv_hbm, wkv), (wr_hbm, wr), (wq_hbm, wq), (uq_hbm, uq), (ukv_hbm, ukv),
+            (freq_hbm, freq_ref), (gq_hbm, gq_ref), (gkv_hbm, gkv_ref),
+        )
     ):
         loads.append(pltpu.make_async_copy(a, b, load_sem.at[n]))
         loads[-1].start()
@@ -63,7 +66,7 @@
     z_peers = [(((z + d) % 8) * 2 + c, t) for d in range(1, 8)]
 
     barrier = pltpu.get_barrier_semaphore()
-    friends = [*along_x[1:], *along_y[1:], sibling] + z_peers
+    friends = [*along_x[1:], *along_y[1:], sibling, z_peers[0], z_peers[6]]
     for who in friends:
         pl.semaphore_signal(barrier, inc=1, device_id=who, device_id_type=MESH)
 
@@ -151,7 +154,17 @@
         part_k[i // 4, i % 4, :, 0:KVL] = pk[rows]
         part_k[i // 4, i % 4, :, KVL:LINE] = pr[rows]
     pl.semaphore_wait(barrier, len(friends))
+
+    def tell(hop):
+        pl.semaphore_signal(near_sem.at[hop, 0], inc=1, device_id=z_peers[0], device_id_type=MESH)
+        pl.semaphore_signal(near_sem.at[hop, 1], inc=1, device_id=z_peers[6], device_id_type=MESH)
+
+    def told(hop):
+        pl.semaphore_wait(near_sem.at[hop, 0], 1)
+        pl.semaphore_wait(near_sem.at[hop, 1], 1)
+
     go(sum_k)
+    tell(0)
 
     loads[3].wait()
     pq = jnp.dot(tokens, wq[...], preferred_element_type=F32)
@@ -160,7 +173,11 @@
     go(sum_q)
     go(sum_k)
     go(sum_q)
+    told(0)
+    tell(1)
     go(sum_k)
+    told(1)
+    tell(2)
     go(sum_q)
     go(sum_k)
     go(sum_q)
@@ -169,6 +186,9 @@
         mean_sq = jnp.sum(v * v, axis=1, keepdims=True) / width
         return (v * lax.rsqrt(mean_sq + EPS) * gain).astype(BF16)
 
+    told(2)
+    for n in (6, 7, 8):
+        loads[n].wait()
     at_run = pos_ref[t * RUN]
     where_at = at_run + lax.broadcasted_iota(jnp.int32, (RUN, 128), 0)
     angle = where_at.astype(F32) * freq_ref[...]
@@ -277,12 +297,9 @@
     for g in gk:
         g.start()
 
-    scale = np.float32((1.0 + 0.1 * np.log(40.0)) ** 2 / np.sqrt(192.0))
+    scale = np.float32((1.0 + 0.1 * np.log(40.0)) ** 2 / np.sqrt(192.0) / np.log(2.0))
     lane8 = lax.broadcasted_iota(jnp.int32, (8, 128), 1)
     pick = jnp.where(lane8 == 64, 64.0, jnp.where(lane8 == 65, 1.0, 0.0)).astype(BF16)
-    m_ref[...] = jnp.full_like(m_ref, -1e30)
-    l_ref[...] = jnp.zeros_like(l_ref)
-    acc_ref[...] = jnp.zeros_like(acc_ref)
     qpos = jnp.concatenate(
         [pos_ref[i * RUN] + lax.broadcasted_iota(jnp.int32, (RUN, 128), 0) for i in range(16)], axis=0
     ).astype(F32)
@@ -311,26 +328,36 @@
                 arrived(ref, k)
                 rows.append(keys[n, p * 4 + q].reshape(128, LINE))
         rows = jnp.concatenate(rows, axis=0)
-        rope_ref[g] = rows[:, KVL:LINE]
-        up_ref[g] = jnp.dot(rows[:, 0:KVL], ukv[...], preferred_element_type=F32).astype(BF16)
-
-    def attend(g):
-        rope_rows = rope_ref[g]
+        spot_g = pl.ds(g * GROUP, GROUP)
+        rope_ref[spot_g] = rows[:, KVL:LINE]
+        up_ref[spot_g] = jnp.dot(rows[:, 0:KVL], ukv[...], preferred_element_type=F32).astype(BF16)
+
+    def attend(g, many):
+        rows = pl.ds(g * GROUP, many * GROUP)
+        rope_rows = rope_ref[rows]
         kpos = lax.dot_general(pick, rope_rows, (((1,), (1,)), ((), ())), preferred_element_type=F32)[0:1]
         seen = kpos <= qcol
         for h in range(HEAD_DEV):
-            kcat = jnp.concatenate([up_ref[g, :, 256 * h : 256 * h + 128], rope_rows], axis=1)
+            kcat = jnp.concatenate([up_ref[rows, 256 * h : 256 * h + 128], rope_rows], axis=1)
             sc = lax.dot_general(qcat[h], kcat, (((1,), (1,)), ((), ())), preferred_element_type=F32)
             sc = jnp.where(seen, sc * scale, -1e30)
-            old = m_ref[h]
-            new = jnp.maximum(old, jnp.max(sc, axis=1, keepdims=True))
-            fade = jnp.exp(old - new)
-            w = jnp.exp(sc - new)
-            m_ref[h] = new
-            l_ref[h] = l_ref[h] * fade + jnp.sum(w, axis=1, keepdims=True)
-            acc_ref[h] = acc_ref[h] * fade + jnp.dot(
-                w.astype(BF16), up_ref[g, :, 256 * h + 128 : 256 * h + 256], preferred_element_type=F32
-            )
+            new = jnp.max(sc, axis=1, keepdims=True)
+            if g:
+                old = m_ref[h]
+                new = jnp.maximum(old, new)
+                fade = jnp.exp2(old - new)
+            w = jnp.exp2(sc - new)
+            mass = jnp.sum(w, axis=1, keepdims=True)
+            mix = jnp.dot(w.astype(BF16), up_ref[rows, 256 * h + 128 : 256 * h + 256], preferred_element_type=F32)
+            if g:
+                mass += l_ref[h] * fade
+                mix += acc_ref[h] * fade
+            if g + many < 8:
+                m_ref[h] = new
+                l_ref[h] = mass
+                acc_ref[h] = mix
+            else:
+                out_ref[:, VDIM * h : VDIM * (h + 1)] = (mix / mass).astype(BF16)
 
     sequence = [(0, 0)]
 
@@ -355,27 +382,28 @@
     q_step((0, 2), (0, 1))
     k_step(2, 1)
     q_step(3)
+    loads[5].wait()
+    expand(0)
     k_step((0, 2), (0, 1), 3)
     q_step((2, 2), (2, 1), (1, 2), (1, 1), (0, 3))
-    loads[5].wait()
-    expand(0)
+    expand(1)
+    expand(2)
     k_step((2, 2), (2, 1), (1, 2), (1, 1))
     q_step((3, 2), (3, 1), (2, 3), (1, 3))
-    expand(1)
+    expand(3)
     k_step((0, 3), (3, 2), (3, 1))
     q_step((3, 3))
     loads[4].wait()
     queries()
-    attend(0)
-    expand(2)
-    attend(1)
+    attend(0, 2)
+    expand(4)
+    attend(2, 2)
     k_step((2, 3), (1, 3), (3, 3))
-    attend(2)
-    for g in range(3, 8):
-        expand(g)
-        attend(g)
-    for h in range(HEAD_DEV):
-        out_ref[:, VDIM * h : VDIM * (h + 1)] = (acc_ref[h] / l_ref[h]).astype(BF16)
+    expand(5)
+    attend(4, 2)
+    expand(6)
+    expand(7)
+    attend(6, 2)
 
     for copy in sent:
         copy.wait_send()
@@ -406,6 +434,7 @@
     tokens, w_rope_key = tokens.T, w_rope_key.T
     scratch = (
         [pltpu.VMEM(a.shape, a.dtype) for a in (tokens, w_down_q, w_down_kv, w_rope_key, w_up_q, w_up_kv)]
+        + [pltpu.VMEM((1, 128), F32), pltpu.VMEM((QL // 128, 128), F32), pltpu.VMEM((1, KVL), F32)]
         + [pltpu.VMEM((4, 4, RUN, QL), F32), pltpu.VMEM((4, 4, RUN, LINE), F32)]
         + [sums((4, RUN), CUTS_Q), sums((4, RUN), CUTS_K), mids(CUTS_Q), mids(CUTS_K)]
         + [sums((RUN,), CUTS_Q), sums((RUN,), CUTS_K)]
@@ -414,21 +443,22 @@
             pltpu.VMEM((RUN, LINE), F32),
             pltpu.VMEM((16, RUN, QL), BF16),
             pltpu.VMEM((2, 16, 2, 4, RUN, LINE), BF16),
-            pltpu.VMEM((8, GROUP, 1024), BF16),
-            pltpu.VMEM((8, GROUP, 128), BF16),
+            pltpu.VMEM((8 * GROUP, 1024), BF16),
+            pltpu.VMEM((8 * GROUP, 128), BF16),
             pltpu.VMEM((HEAD_DEV, 256, 256), BF16),
             pltpu.VMEM((HEAD_DEV, 256, 1), F32),
             pltpu.VMEM((HEAD_DEV, 256, 1), F32),
             pltpu.VMEM((HEAD_DEV, 256, VDIM), F32),
-            pltpu.SemaphoreType.DMA((6,)),
+            pltpu.SemaphoreType.DMA((9,)),
             pltpu.SemaphoreType.DMA((SEMS,)),
             pltpu.SemaphoreType.DMA((SEMS,)),
+            pltpu.SemaphoreType.REGULAR((3, 2)),
         ]
     )
     return pl.pallas_call(
         kernel,
         out_shape=jax.ShapeDtypeStruct((256, HEAD_DEV * VDIM), BF16),
-        in_specs=[smem, vmem, vmem, vmem] + [any_] * 6,
+        in_specs=[smem] + [any_] * 9,
         out_specs=vmem,
         scratch_shapes=scratch,
         compiler_params=pltpu.CompilerParams(

time: 73.8 us -> 69.2 us (0.938)
  the two profiles are of different devices: /device:TPU:6 before, /device:TPU:1 now
where the time goes in v3:
time: 69.2 us; the launch traced here: 69.1 us
  Pallas kernels  67.4 us (97%)
  local copies, waits for them, and re-layouts  1.67 us (2%)
    pallas_call x1, Pallas kernels, body(): pl.pallas_call(kernel, out_shape=jax.ShapeDtypeStruct((256, HEAD_DEV * VD...  67.4 us
    unnamed x1, local copies, waits for them, and re-layouts  1.67 us

profile of v3, /device:TPU:1, one launch (start us, length us, event | category | flops | bytes accessed | tf_op | source)
XLA Modules:
  0.0 69.1 jit_solution(11661571534838728370)
XLA Ops:
  0.0 67.4 %shard_map.100 = bf16[256,512]{1,0:T(8,128)(2,1)} custom-call(s32[256]{0:T(256)} %pos_ref.1, f32[1,128]{1,0:T(1,128)} %constant.2.clone.freq_hbm, f32[12,128]{1,0:T(8,128)} %bitcast.6, f32[1,512]{1,0:T(1,128)} %bitcast.7, bf16[448,256]{1,0:T(8,128)(2,1)} %bitcast.4, bf16[448,1536]{1,0:T(8,128)(2,1)} %wq_hbm.1, bf16[448,512]{1,0:T(8,128)(2,1)} %wkv_hbm.1, ...), custom_call_target="tpu_custom_call" | custom-call | tf_op jit(solution)/shard_map/pallas_call | solution.py:458
  67.4 1.7 %copy.12 = bf16[256,512]{1,0:T(8,128)(2,1)} copy(bf16[256,512]{1,0:T(8,128)(2,1)} %shard_map.100) | data formatting | bytes 524288
